TPU v7x, 32 devices: a whole 2x2x4 slice. The times are simulated.
32 devices in a mesh: row: 4 (over y, x), col: 8 (over z, core).
Axes of the slice: x: 2, y: 2, z: 4, core: 2. Of those that a mesh axis runs over, the one named last changes fastest.
Arguments:
- anc_inverse: float32 [10240, 10240], P('row', 'col'), may hold values from -0.0625 to 0.0625
- lower_anc: float32 [10240, 3, 384], P('col', None, 'row'), may hold values from -1.5 to 1.5
- upper_anc: float32 [10240, 3, 384], P('row', None, 'col'), may hold values from -0.75 to 0.75
- lower_edge: float32 [2, 384, 384], replicated, may hold values from -0.3125 to 0.3125
- upper_edge: float32 [2, 384, 384], replicated, may hold values from -0.3125 to 0.3125
- diag_inverse: float32 [3, 384, 384], replicated, may hold values from -6 to 6
- tile_mask: int32 [3, 80, 3], replicated, may hold values 0 or 1
Outputs:
- x_blocks: float32 [10240, 3, 384], P(('row', 'col'))
- y_blocks: float32 [8, 4, 320, 3, 384], P('col', 'row')
- z_blocks: float32 [3, 384, 384], P(None, 'row', 'col')
- cross_blocks: float32 [2, 2, 384, 384], P(None, None, 'row', 'col')
All inputs are finite; a program needn't handle non-finite values.
Results may differ from a plain program's by a relative error of at most 0.0001.
Values sent between devices are 32-bit elements; how exact they have to be, the bound alone decides.
A program may use at most 128 MiB of HBM per device.

v0:
```python
import jax
import jax.numpy as jnp
from jax import lax
from jax.sharding import PartitionSpec as P

W = 384
BLK = 128
SUPER = 3
precise = lax.Precision.HIGHEST


def product(left, right):
    return jnp.dot(left, right, precision=precise, preferred_element_type=jnp.float32)


def inner_product(left, right):
    return lax.dot_general(
        left, right, (((0,), (0,)), ((), ())), precision=precise, preferred_element_type=jnp.float32
    )


def outer_product(left, right):
    return lax.dot_general(
        left, right, (((1,), (1,)), ((), ())), precision=precise, preferred_element_type=jnp.float32
    )


def tile_pattern(tile_mask, first_block, blocks):
    window = lax.dynamic_slice_in_dim(tile_mask, first_block, blocks, 1).astype(jnp.float32)
    window = jnp.transpose(window, (1, 0, 2))
    widened = jnp.broadcast_to(window[:, None, :, :, None], (blocks, BLK, SUPER, W // BLK, BLK))
    return widened.reshape(blocks * BLK, SUPER, W)


def row_term(anc_inverse, lower_cols):
    return product(anc_inverse, lower_cols)


def col_term(anc_inverse, upper_rows):
    return inner_product(anc_inverse, upper_rows)


def per_device(anc_inverse, lower_anc, upper_anc, lower_edge, upper_edge, diag_inverse, tile_mask):
    rows_here, cols_here = anc_inverse.shape
    slab_rows = rows_here // lax.axis_size("col")
    row_index = lax.axis_index("row")
    col_index = lax.axis_index("col")
    col_pattern = tile_pattern(tile_mask, col_index * (cols_here // BLK), cols_here // BLK)
    row_pattern = tile_pattern(tile_mask, row_index * (rows_here // BLK), rows_here // BLK)
    lower_list = []
    upper_list = []
    cols_list = []
    rows_list = []
    lower_full = lax.all_gather(lower_anc, "row", axis=2, tiled=True) * col_pattern
    upper_full = lax.all_gather(upper_anc, "col", axis=2, tiled=True) * row_pattern
    cols_all = lax.psum_scatter(
        row_term(anc_inverse, lower_full.reshape(cols_here, SUPER * W)),
        "col",
        scatter_dimension=0,
        tiled=True,
    )
    rows_all = lax.psum_scatter(
        col_term(anc_inverse, upper_full.reshape(rows_here, SUPER * W)),
        "row",
        scatter_dimension=0,
        tiled=True,
    )
    cols_all = cols_all.reshape(slab_rows, SUPER, W)
    rows_all = rows_all.reshape(slab_rows, SUPER, W)
    for node_index in range(SUPER):
        lower_list.append(lower_full[:, node_index, :])
        upper_list.append(upper_full[:, node_index, :])
        cols_list.append(cols_all[:, node_index, :])
        rows_list.append(rows_all[:, node_index, :])
    x_list = []
    y_list = []
    corner_list = []
    cross_cols = []
    cross_rows = []
    for node_index in range(SUPER):
        lower_cur = lower_list[node_index]
        upper_cur = upper_list[node_index]
        inv_cols = -cols_list[node_index]
        inv_rows = -rows_list[node_index]
        upper_mine = lax.dynamic_slice_in_dim(upper_cur, col_index * slab_rows, slab_rows, 0)
        if node_index > 0:
            lower_side = lower_edge[node_index - 1]
            upper_side = upper_edge[node_index - 1]
            lower_mine = lax.dynamic_slice_in_dim(lower_cur, row_index * slab_rows, slab_rows, 0)
            rows_lower = inner_product(prev_rows, lower_mine)
            upper_cols = inner_product(upper_mine, prev_cols)
        if node_index > 0:
            rows_lower, upper_cols = lax.psum((rows_lower, upper_cols), ("row", "col"))
        if node_index > 0:
            cross_col = -(rows_lower + product(prev_corner, lower_side))
            cross_row = -(upper_cols + product(upper_side, prev_corner))
            inv_cols = inv_cols - product(prev_cols, lower_side)
            inv_rows = inv_rows - outer_product(prev_rows, upper_side)
            cross_cols.append(cross_col)
            cross_rows.append(cross_row)
        inv_corner = diag_inverse[node_index] - lax.psum(
            inner_product(upper_mine, inv_cols), ("row", "col")
        )
        if node_index > 0:
            inv_corner = inv_corner - product(upper_side, cross_col)
        x_list.append(inv_cols)
        y_list.append(inv_rows)
        corner_list.append(inv_corner)
        prev_cols = inv_cols
        prev_rows = inv_rows
        prev_corner = inv_corner
    x_blocks = jnp.stack(x_list, axis=1)
    y_blocks = jnp.stack(y_list, axis=1)[None, None]
    tile_rows = W // lax.axis_size("row")
    tile_cols = W // lax.axis_size("col")
    corners = jnp.stack(corner_list)
    corners = lax.dynamic_slice_in_dim(corners, row_index * tile_rows, tile_rows, 1)
    z_blocks = lax.dynamic_slice_in_dim(corners, col_index * tile_cols, tile_cols, 2)
    crossed = jnp.stack([jnp.stack(cross_cols), jnp.stack(cross_rows)])
    crossed = lax.dynamic_slice_in_dim(crossed, row_index * tile_rows, tile_rows, 2)
    cross_blocks = lax.dynamic_slice_in_dim(crossed, col_index * tile_cols, tile_cols, 3)
    return (x_blocks, y_blocks, z_blocks, cross_blocks)


def solution(mesh):
    return jax.shard_map(
        per_device,
        mesh=mesh,
        in_specs=(
            P("row", "col"),
            P("col", None, "row"),
            P("row", None, "col"),
            P(),
            P(),
            P(),
            P(),
        ),
        out_specs=(
            P(("row", "col"), None, None),
            P("col", "row", None, None, None),
            P(None, "row", "col"),
            P(None, None, "row", "col"),
        ),
        check_vma=False,
    )
```

profile of v0, /device:TPU:0, one launch (start us, length us, event | category | flops | bytes accessed | tf_op | source)
XLA Modules:
  0.0 565.6 jit_solution(17613502817447202190)
XLA Ops:
  7.2 0.7 all-gather.3.cloned.1.call-update
  8.0 0.7 all-gather.5.cloned.1.call-update
  8.8 0.1 copy.69
  8.9 4.2 broadcast_in_dim.6
  13.1 10.5 %reshape.42 = f32[1280,3,384]{2,0,1:T(8,128)} reshape(f32[10,128,3,3,128]{4,3,1,0,2:T(4,128)} %broadcast_in_dim.6) | data formatting | bytes 11796480 | tf_op jit(solution)/shard_map/reshape | solution.py:32
  23.6 55.8 %all-gather.3.cloned.1.call-done = f32[1280,3,384]{0,2,1:T(8,128)} async-done(((f32[1280,3,96]{0,2,1:T(8,128)}), f32[1280,3,384]{0,2,1:T(8,128)}) %all-gather.3.cloned.1.call-update) | async-done | bytes 5898256 | tf_op jit(solution)/shard_map/all_gather | solution.py:54
  79.3 7.7 %copy.70 = f32[1280,3,384]{2,0,1:T(8,128)} copy(f32[1280,3,384]{0,2,1:T(8,128)} %all-gather.3.cloned.1.call-done) | data formatting | bytes 11796480 | tf_op jit(solution)/shard_map/all_gather | solution.py:54
  87.0 9.3 %mul.30 = f32[1280,3,384]{2,0,1:T(8,128)} multiply(f32[1280,3,384]{2,0,1:T(8,128)} %copy.70, f32[1280,3,384]{2,0,1:T(8,128)} %reshape.42) | non-fusion elementwise | flops 1474560 | bytes 17694720 | tf_op jit(solution)/shard_map/mul | solution.py:54
  96.3 7.8 %copy.71 = f32[1280,3,384]{0,2,1:T(8,128)} copy(f32[1280,3,384]{2,0,1:T(8,128)} %mul.30) | data formatting | bytes 11796480 | tf_op jit(solution)/shard_map/mul | solution.py:54
  104.0 52.7 %convolution_bitcast_fusion = f32[2560,1152]{0,1:T(8,128)} fusion(f32[1280,1152]{0,1:T(8,128)} %bitcast.163, f32[2560,1280]{1,0:T(8,128)} %param.7), kind=kOutput, calls=%fused_computation | convolution fusion | flops 45298483200 | bytes 30801920 | tf_op jit(solution)/shard_map/dot_general | solution.py:13
  156.8 13.6 %copy.92 = f32[2560,1152]{1,0:T(8,128)} copy(f32[2560,1152]{0,1:T(8,128)} %convolution_bitcast_fusion) | data formatting | bytes 23592960
  170.4 0.6 reduce-scatter.9.cloned.1.call-start
  171.1 6.0 %broadcast_in_dim.7 = f32[20,128,3,3,128]{1,0,4,3,2:T(8,128)} broadcast(f32[20,3,3]{0,2,1:T(4,128)S(1)} %convert_bitcast_fusion), dimensions={0,2,3} | broadcast | bytes 11797200 | tf_op jit(solution)/shard_map/broadcast_in_dim | solution.py:31
  177.1 13.7 %reshape.45 = f32[2560,3,384]{0,2,1:T(8,128)} reshape(f32[20,128,3,3,128]{1,0,4,3,2:T(8,128)} %broadcast_in_dim.7) | data formatting | bytes 23592960 | tf_op jit(solution)/shard_map/reshape | solution.py:32
  190.8 0.4 all-gather.5.cloned.1.call-done
  191.2 9.7 %mul.32 = f32[2560,3,384]{0,2,1:T(8,128)S(1)} multiply(f32[2560,3,384]{0,2,1:T(8,128)} %all-gather.5.cloned.1.call-done, f32[2560,3,384]{0,2,1:T(8,128)} %reshape.45) | non-fusion elementwise | flops 2949120 | bytes 35389440 | tf_op jit(solution)/shard_map/mul | solution.py:55
  200.9 4.3 copy-done
  205.3 50.1 %convolution_bitcast_fusion.1 = f32[1280,1152]{0,1:T(8,128)} fusion(f32[2560,1152]{0,1:T(8,128)S(1)} %bitcast.157, f32[2560,1280]{1,0:T(8,128)} %param.7), kind=kOutput, calls=%fused_computation.1 | convolution fusion | flops 45298483200 | bytes 30801920 | tf_op jit(solution)/shard_map/dot_general | solution.py:17
  255.4 7.7 %copy.94 = f32[1280,1152]{1,0:T(8,128)} copy(f32[1280,1152]{0,1:T(8,128)} %convolution_bitcast_fusion.1) | data formatting | bytes 11796480
  263.1 0.2 all-reduce.3.cloned.1.call-start
  263.3 4.3 fusion.75
  267.6 9.3 %fusion.74 = (f32[2560,1,384]{0,2,1:T(8,128)}, f32[2560,1,384]{0,2,1:T(8,128)}, f32[2560,1,384]{0,2,1:T(8,128)}) fusion(f32[2560,3,384]{0,2,1:T(8,128)} %copy-done), kind=kLoop, calls=%fused_computation.100 | loop fusion | bytes 23592960 | tf_op jit(solution)/shard_map/slice | solution.py:72
  276.9 36.6 %reduce-scatter.7.cloned.1.call-done = f32[320,1152]{1,0:T(8,128)} async-done(((f32[2560,1152]{1,0:T(8,128)}), f32[320,1152]{1,0:T(8,128)}) %reduce-scatter.7.cloned.1.call-update) | async-done | bytes 1474576
  313.5 2.1 copy.93
  315.6 0.9 fusion.77
  316.6 1.3 copy.96
  317.8 1.0 copy.97
  318.8 0.2 copy.98
  319.1 3.3 fusion.16
  322.4 1.1 convolution_subtract_fusion.3
  323.5 3.3 fusion.18
  326.7 3.3 fusion.12
  330.0 1.1 convolution_subtract_fusion.2
  331.1 0.8 copy-done.6
  331.9 3.2 fusion.14
  335.1 46.5 %reduce-scatter.9.cloned.1.call-done = f32[320,1152]{1,0:T(8,128)} async-done(((f32[1280,1152]{1,0:T(8,128)}), f32[320,1152]{1,0:T(8,128)}) %reduce-scatter.9.cloned.1.call-update) | async-done | bytes 1474576
  381.6 2.3 copy.95
  384.0 1.3 fusion.76
  385.2 1.4 copy.99
  386.6 2.1 copy.100
  388.7 3.3 fusion.20
  392.0 1.1 convolution_subtract_fusion.1
  393.1 3.2 fusion.49
  396.3 3.2 fusion.47
  399.5 0.8 neg.53
  400.4 0.8 neg.59
  401.2 1.3 copy.101
  402.5 2.2 pad_maximum_fusion
  404.7 1.1 fusion.11
  405.8 1.2 maximum_bitcast_fusion
  407.0 137.7 %all-reduce.3.cloned.1.call-done = (f32[384,384]{1,0:T(8,128)}, f32[384,384]{1,0:T(8,128)}, f32[384,384]{1,0:T(8,128)}, f32[384,384]{1,0:T(8,128)}, f32[384,384]...) async-done(((f32[384,384]{1,0:T(8,128)}, f32[384,384]{1,0:T(8,128)}, f32[384,384]{1,0:T(8,128)}, f32[384,384]{1,0:T(8,128)}, f32[384,384]{1,0:T(8,128)}, ...) | async-done | bytes 4128784 | tf_op jit(solution)/shard_map/psum | solution.py:101
  544.7 1.4 fusion.73
  546.2 0.1 copy-done.15
  546.3 2.5 fusion.7
  548.9 1.3 fusion
  550.2 1.3 fusion.10
  551.5 1.6 fusion.4
  553.1 1.3 fusion.1
  554.3 0.2 maximum_bitcast_fusion.1
  554.5 0.1 fusion.58
  554.7 0.7 copy.85
  555.4 2.5 fusion.9
  557.9 0.1 fusion.60
  558.1 0.7 copy.84
  (39 shorter events, 0.4 us)
Async XLA Ops:
  7.2 1.5 copy-start.16
  7.2 72.2 %all-gather.3.cloned.1.call-start = ((), (), s32[]{:S(2)}) async-start(), calls=%async_computation.2 | async-start | bytes 7372800 | tf_op jit(solution)/shard_map/all_gather | solution.py:54
  7.9 183.3 %all-gather.5.cloned.1.call-start = ((), (), s32[]{:S(2)}) async-start(), calls=%async_computation.3 | async-start | bytes 13271040 | tf_op jit(solution)/shard_map/all_gather | solution.py:55
  8.7 304.8 %reduce-scatter.7.cloned.1.call-start = ((), (), s32[]{:S(2)}) async-start(), calls=%async_computation.4 | async-start | bytes 13271040
  170.4 211.2 %reduce-scatter.9.cloned.1.call-start = ((), (), s32[]{:S(2)}) async-start(), calls=%async_computation.5 | async-start | bytes 7372800
  200.9 4.3 copy-start
  263.1 281.6 %all-reduce.3.cloned.1.call-start = ((), (), s32[]{:S(2)}) async-start(), calls=%async_computation.6 | async-start | bytes 8257536 | tf_op jit(solution)/shard_map/psum | solution.py:101
  317.8 4.5 copy-start.4
  319.1 3.3 copy-start.9
  331.1 0.8 copy-start.6
  385.2 6.8 %copy-start.1 = (f32[2,384,384]{2,1,0:T(8,128)S(1)}, f32[2,384,384]{2,1,0:T(8,128)}, u32[]{:S(2)}) copy-start(f32[2,384,384]{2,1,0:T(8,128)} %param.11) | copy-start | bytes 3538948
  388.7 3.3 copy-start.10
  400.4 2.1 copy-start.7
  404.7 1.1 copy-start.8
  544.7 1.5 copy-start.2
  544.7 1.6 copy-start.15
  544.7 4.2 copy-start.14
  546.1 2.7 copy-start.3
  546.1 2.7 copy-start.5
  548.8 1.3 copy-start.13
  550.1 1.3 copy-start.12
  551.5 1.6 copy-start.11
Sparse Core Ops, SparseCore 0:
  9.8 69.4 all-gather.2
  81.0 110.1 all-gather.4
  193.5 119.9 reduce-scatter.6
  316.4 65.2 reduce-scatter.8
  399.6 144.9 all-reduce.2
where the time goes:
time: 574 us; the launch traced here: 566 us
  waiting for transfers between devices  278 us (48%)
  matrix products  140 us (24%)
  local copies, waits for them, and re-layouts  105 us (18%)
  other arithmetic  26.1 us (5%)
  between operations  14.4 us (3%)
    psum x1, waiting for transfers between devices, per_device(): lax.psum(inner_product(upper_mine, inv_cols), ('row', 'col'))  138 us
    unnamed x7, waiting for transfers between devices  84.6 us
    dot_general x8, matrix products, inner_product(): lax.dot_general(left, right, (((0,), (0,)), ((), ())), precision=precise,...  72.9 us
    dot_general x9, matrix products, product(): jnp.dot(left, right, precision=precise, preferred_element_type=jnp.float32)  65.3 us
    all_gather x1, waiting for transfers between devices, per_device(): lax.all_gather(lower_anc, 'row', axis=2, tiled=True) * col_pattern  55.8 us
    unnamed x46, local copies, waits for them, and re-layouts  39.8 us
    reshape x2, local copies, waits for them, and re-layouts, tile_pattern(): return widened.reshape(blocks * BLK, SUPER, W)  24.2 us
  transfers between devices with their start and end apart: 5, of which 5 were waited for; matrix products, arithmetic and copies ran while one was open for 42% of the time, Pallas kernels for 0%

commit v1 on v0

--- a/solution.py
+++ b/solution.py
@@ -99,7 +99,7 @@
             cross_cols.append(cross_col)
             cross_rows.append(cross_row)
         inv_corner = diag_inverse[node_index] - lax.psum(
-            inner_product(upper_mine, inv_cols), ("row", "col")
+            lax.psum(inner_product(upper_mine, inv_cols), "col"), "row"
         )
         if node_index > 0:
             inv_corner = inv_corner - product(upper_side, cross_col)

time: 574 us -> 703 us (1.22)
  waiting for transfers between devices: 278 us -> 402 us
    unnamed x7 -> x9, waiting for transfers between devices: 84.6 us -> 165 us
    psum x1 -> x3, waiting for transfers between devices: 138 us -> 180 us  [the longest x1 140 us: per_device(): rows_lower, upper_cols = lax.psum((rows_lower, upper_cols), ('row', 'col'))]
    unnamed x46 -> x44, local copies, waits for them, and re-layouts: 39.8 us -> 34.3 us
  transfers between devices with their start and end apart: 5 -> 7, of which waited for: 5 -> 7; matrix products, arithmetic and copies ran while one was open for 42% -> 35% of each run, Pallas kernels for 0% -> 0%
where the time goes in v1:
time: 703 us; the launch traced here: 695 us
  waiting for transfers between devices  402 us (57%)
  matrix products  146 us (21%)
  local copies, waits for them, and re-layouts  99.8 us (14%)
  other arithmetic  31.3 us (4%)
  between operations  14.7 us (2%)
    unnamed x9, waiting for transfers between devices  165 us
    psum x1, waiting for transfers between devices, per_device(): rows_lower, upper_cols = lax.psum((rows_lower, upper_cols), ('row', 'col'))  140 us
    dot_general x8, matrix products, inner_product(): lax.dot_general(left, right, (((0,), (0,)), ((), ())), precision=precise,...  75.9 us
    dot_general x9, matrix products, product(): jnp.dot(left, right, precision=precise, preferred_element_type=jnp.float32)  67.6 us
    all_gather x1, waiting for transfers between devices, per_device(): lax.all_gather(lower_anc, 'row', axis=2, tiled=True) * col_pattern  55.8 us
    psum x1, waiting for transfers between devices, per_device(): lax.psum(lax.psum(inner_product(upper_mine, inv_cols), 'col'), 'row')  39.1 us
    unnamed x44, local copies, waits for them, and re-layouts  34.3 us
    reshape x2, local copies, waits for them, and re-layouts, tile_pattern(): return widened.reshape(blocks * BLK, SUPER, W)  24.2 us
  transfers between devices with their start and end apart: 7, of which 7 were waited for; matrix products, arithmetic and copies ran while one was open for 35% of the time, Pallas kernels for 0%

profile of v1, /device:TPU:0, one launch (start us, length us, event | category | flops | bytes accessed | tf_op | source)
XLA Modules:
  0.0 694.6 jit_solution(81587714710747010)
XLA Ops:
  7.2 0.7 all-gather.3.cloned.1.call-update
  8.0 0.7 all-gather.5.cloned.1.call-update
  8.7 0.1 convert_bitcast_fusion.1
  8.8 0.1 copy.69
  8.9 4.1 broadcast_in_dim.6
  13.0 10.5 %reshape.42 = f32[1280,3,384]{2,0,1:T(8,128)} reshape(f32[10,128,3,3,128]{4,3,1,0,2:T(4,128)} %broadcast_in_dim.6) | data formatting | bytes 11796480 | tf_op jit(solution)/shard_map/reshape | solution.py:32
  23.5 55.8 %all-gather.3.cloned.1.call-done = f32[1280,3,384]{0,2,1:T(8,128)} async-done(((f32[1280,3,96]{0,2,1:T(8,128)}), f32[1280,3,384]{0,2,1:T(8,128)}) %all-gather.3.cloned.1.call-update) | async-done | bytes 5898256 | tf_op jit(solution)/shard_map/all_gather | solution.py:54
  79.3 7.7 %copy.70 = f32[1280,3,384]{2,0,1:T(8,128)} copy(f32[1280,3,384]{0,2,1:T(8,128)} %all-gather.3.cloned.1.call-done) | data formatting | bytes 11796480 | tf_op jit(solution)/shard_map/all_gather | solution.py:54
  87.0 9.3 %mul.30 = f32[1280,3,384]{2,0,1:T(8,128)} multiply(f32[1280,3,384]{2,0,1:T(8,128)} %copy.70, f32[1280,3,384]{2,0,1:T(8,128)} %reshape.42) | non-fusion elementwise | flops 1474560 | bytes 17694720 | tf_op jit(solution)/shard_map/mul | solution.py:54
  96.3 7.8 %copy.71 = f32[1280,3,384]{0,2,1:T(8,128)} copy(f32[1280,3,384]{2,0,1:T(8,128)} %mul.30) | data formatting | bytes 11796480 | tf_op jit(solution)/shard_map/mul | solution.py:54
  104.1 52.7 %convolution_bitcast_fusion = f32[2560,1152]{0,1:T(8,128)} fusion(f32[1280,1152]{0,1:T(8,128)} %bitcast.163, f32[2560,1280]{1,0:T(8,128)} %param.7), kind=kOutput, calls=%fused_computation | convolution fusion | flops 45298483200 | bytes 30801920 | tf_op jit(solution)/shard_map/dot_general | solution.py:13
  156.7 13.5 %copy.92 = f32[2560,1152]{1,0:T(8,128)} copy(f32[2560,1152]{0,1:T(8,128)} %convolution_bitcast_fusion) | data formatting | bytes 23592960
  170.3 0.6 all-reduce.9.cloned.1.call-start
  170.9 6.0 broadcast_in_dim.7
  177.0 13.7 %reshape.45 = f32[2560,3,384]{0,2,1:T(8,128)} reshape(f32[20,128,3,3,128]{1,0,4,3,2:T(8,128)} %broadcast_in_dim.7) | data formatting | bytes 23592960 | tf_op jit(solution)/shard_map/reshape | solution.py:32
  190.7 0.5 all-gather.5.cloned.1.call-done
  191.2 14.1 %mul.32 = f32[2560,3,384]{0,2,1:T(8,128)} multiply(f32[2560,3,384]{0,2,1:T(8,128)} %all-gather.5.cloned.1.call-done, f32[2560,3,384]{0,2,1:T(8,128)} %reshape.45) | non-fusion elementwise | flops 2949120 | bytes 35389440 | tf_op jit(solution)/shard_map/mul | solution.py:55
  205.3 9.1 %fusion.74 = (f32[2560,1,384]{0,2,1:T(8,128)}, f32[2560,1,384]{0,2,1:T(8,128)}, f32[2560,1,384]{0,2,1:T(8,128)}) fusion(f32[2560,3,384]{0,2,1:T(8,128)} %mul.32), kind=kLoop, calls=%fused_computation.100 | loop fusion | bytes 23592960 | tf_op jit(solution)/shard_map/slice | solution.py:72
  214.4 99.1 %reduce-scatter.7.cloned.1.call-done = f32[320,1152]{1,0:T(8,128)} async-done(((f32[2560,1152]{1,0:T(8,128)}), f32[320,1152]{1,0:T(8,128)}) %reduce-scatter.7.cloned.1.call-update) | async-done | bytes 1474576
  313.5 2.1 copy.93
  315.6 0.9 fusion.77
  316.6 1.4 copy.96
  317.9 1.0 copy.97
  318.9 0.2 copy.98
  319.2 2.1 convolution_subtract_fusion.3
  321.3 1.1 convolution_subtract_fusion.2
  322.4 3.4 fusion.18
  325.8 3.2 fusion.20
  329.1 3.2 fusion.14
  332.3 0.2 reduce-scatter.9.cloned.1.call-start
  332.5 52.9 %convolution_bitcast_fusion.1 = f32[1280,1152]{0,1:T(8,128)} fusion(f32[2560,1152]{0,1:T(8,128)} %bitcast.157, f32[2560,1280]{1,0:T(8,128)} %param.7), kind=kOutput, calls=%fused_computation.1 | convolution fusion | flops 45298483200 | bytes 30801920 | tf_op jit(solution)/shard_map/dot_general | solution.py:17
  385.4 7.7 %copy.94 = f32[1280,1152]{1,0:T(8,128)} copy(f32[1280,1152]{0,1:T(8,128)} %convolution_bitcast_fusion.1) | data formatting | bytes 11796480
  393.2 1.1 all-reduce.9.cloned.1.call-done
  394.4 4.3 fusion.75
  398.7 64.9 %reduce-scatter.9.cloned.1.call-done = f32[320,1152]{1,0:T(8,128)} async-done(((f32[1280,1152]{1,0:T(8,128)}), f32[320,1152]{1,0:T(8,128)}) %reduce-scatter.9.cloned.1.call-update) | async-done | bytes 1474576
  463.6 2.3 copy.95
  465.9 1.1 fusion.76
  467.0 1.3 copy.99
  468.3 1.0 copy.100
  469.3 3.3 fusion.12
  472.6 3.4 fusion.16
  476.0 3.2 fusion.49
  479.1 1.1 convolution_subtract_fusion.1
  480.2 3.3 fusion.47
  483.5 0.8 neg.53
  484.3 0.9 neg.59
  485.2 2.1 copy.101
  487.3 2.3 pad_maximum_fusion
  489.6 1.1 fusion.11
  490.7 1.2 maximum_bitcast_fusion
  491.9 39.1 %all-reduce.11.cloned.1.call-done = (f32[384,384]{1,0:T(8,128)}, f32[384,384]{1,0:T(8,128)}, f32[384,384]{1,0:T(8,128)}) async-done(((f32[384,384]{1,0:T(8,128)}, f32[384,384]{1,0:T(8,128)}, f32[384,384]{1,0:T(8,128)}), (f32[384,384]{1,0:T(8,128)}, f32[384,384]{1,0:T(8,128)}, f32[384,384]{1,0:T(8,128)})) %all-reduce.11.cloned.1.call-update) | async-done | bytes 1769488 | tf_op jit(solution)/shard_map/psum | solution.py:101
  531.0 2.2 fusion.73
  533.2 140.4 %all-reduce.7.cloned.1.call-done = (f32[384,384]{1,0:T(8,128)}, f32[384,384]{1,0:T(8,128)}, f32[384,384]{1,0:T(8,128)}, f32[384,384]{1,0:T(8,128)}) async-done(((f32[384,384]{1,0:T(8,128)}, f32[384,384]{1,0:T(8,128)}, f32[384,384]{1,0:T(8,128)}, f32[384,384]{1,0:T(8,128)}), (f32[384,384]{1,0:T(8,128)}, f32[384,384]{1,0:T(8,128)}, f32[384,384]{1,0:T(8,128)}, ...) | async-done | bytes 2359312 | tf_op jit(solution)/shard_map/psum | solution.py:93
  673.6 2.7 fusion.7
  676.3 2.4 fusion
  678.8 1.6 fusion.10
  680.4 1.3 fusion.4
  681.8 1.3 fusion.1
  683.0 0.2 maximum_bitcast_fusion.1
  683.2 0.1 fusion.58
  683.4 0.7 copy.85
  684.1 2.5 fusion.9
  686.7 0.1 fusion.60
  686.8 0.7 copy.84
  (43 shorter events, 0.5 us)
Async XLA Ops:
  7.2 1.5 copy-start.15
  7.2 72.2 %all-gather.3.cloned.1.call-start = ((), (), s32[]{:S(2)}) async-start(), calls=%async_computation.2 | async-start | bytes 7372800 | tf_op jit(solution)/shard_map/all_gather | solution.py:54
  7.9 183.3 %all-gather.5.cloned.1.call-start = ((), (), s32[]{:S(2)}) async-start(), calls=%async_computation.3 | async-start | bytes 13271040 | tf_op jit(solution)/shard_map/all_gather | solution.py:55
  8.7 304.8 %reduce-scatter.7.cloned.1.call-start = ((), (), s32[]{:S(2)}) async-start(), calls=%async_computation.4 | async-start | bytes 13271040
  170.3 224.0 %all-reduce.9.cloned.1.call-start = ((), (), s32[]{:S(2)}) async-start(), calls=%async_computation.7 | async-start | bytes 3538944 | tf_op jit(solution)/shard_map/psum | solution.py:102
  316.6 2.6 copy-start.3
  322.4 6.7 copy-start.6
  332.3 131.2 %reduce-scatter.9.cloned.1.call-start = ((), (), s32[]{:S(2)}) async-start(), calls=%async_computation.5 | async-start | bytes 7372800
  393.2 137.8 %all-reduce.11.cloned.1.call-start = ((), (), s32[]{:S(2)}) async-start(), calls=%async_computation.8 | async-start | bytes 3538944 | tf_op jit(solution)/shard_map/psum | solution.py:101
  394.3 279.3 %all-reduce.7.cloned.1.call-start = ((), (), s32[]{:S(2)}) async-start(), calls=%async_computation.6 | async-start | bytes 4718592 | tf_op jit(solution)/shard_map/psum | solution.py:93
  472.6 6.5 copy-start
  472.6 6.5 copy-start.10
  484.3 3.0 copy-start.7
  487.3 2.3 copy-start.11
  489.6 1.1 copy-start.9
  531.0 142.6 %copy-start.1 = (f32[384,384]{1,0:T(8,128)S(1)}, f32[384,384]{1,0:T(8,128)}, u32[]{:S(2)}) copy-start(f32[384,384]{1,0:T(8,128)} %get-tuple-element.31) | copy-start | bytes 1769476
  533.2 143.1 %copy-start.4 = (f32[2,384,384]{2,1,0:T(8,128)S(1)}, f32[2,384,384]{2,1,0:T(8,128)}, u32[]{:S(2)}) copy-start(f32[2,384,384]{2,1,0:T(8,128)} %param.10) | copy-start | bytes 3538948
  673.6 2.7 copy-start.2
  676.3 2.4 copy-start.12
  678.7 1.6 copy-start.14
  680.3 1.3 copy-start.5
  680.3 1.4 copy-start.13
  683.4 3.3 copy-start.8
Sparse Core Ops, SparseCore 0:
  9.8 69.4 all-gather.2
  81.0 110.1 all-gather.4
  193.5 119.9 reduce-scatter.6
  332.4 61.7 all-reduce.8
  397.1 66.3 reduce-scatter.8
  466.9 64.1 all-reduce.10
  537.0 136.5 all-reduce.6
